TPU v7x, 512 devices: a whole 4x8x8 slice. The times are simulated.
512 devices in a mesh: val: 64 (over z_hi, y, core), qry: 8 (over z_lo, x).
Axes of the slice: x: 4, y: 8, z: 8 (z_hi: 4, z_lo: 2; z = z_hi * 2 + z_lo), core: 2. Of those that a mesh axis runs over, the one named last changes fastest.
Arguments:
- queries: bfloat16 [12288, 512], P('qry'), may hold values from -20 to 20
- pool_keys: bfloat16 [32768, 512], P('val'), may hold values from -20 to 20
- pool_values: bfloat16 [32768, 512], P('val'), may hold values from -6 to 6
- out_grad: bfloat16 [12288, 512], P('qry'), may hold values from -6 to 6
- lse: float32 [2, 12288], P(None, 'qry'), as said below
- compat: int32 [2, 64, 48], P(None, 'val', 'qry'), may hold values from 0 to 1, as said below
- targets: int32 [12288, 2], P('qry'), may hold values from 0 to 32767
Outputs:
- query_grad: bfloat16 [12288, 512], P('qry')
- key_grad: bfloat16 [32768, 512], P(('val', 'qry'))
- value_grad: bfloat16 [32768, 512], P(('val', 'qry'))
Inputs may be any that keep to these rules, and one draw needn't show every extreme that they name: `lse`: the forward pass's value: the log of the sum over allowed j of exp(scores[h, i, j]). `compat`: 1 where a block of 512 pool values and a block of 256 queries are type-compatible for that head.
All inputs are finite; a program needn't handle non-finite values.
Results may differ from a plain program's by a relative error of at most 0.0053.
Values may be sent and summed in bfloat16 or wider, within the bound.
A program may use at most 128 MiB of HBM per device.

v0:
```python
from functools import partial

import jax
import jax.numpy as jnp
from jax import lax
from jax.sharding import PartitionSpec as P


def on_device(queries, pool_keys, pool_values, out_grad, lse, compat, targets):
    num_heads = compat.shape[0]
    head_width = queries.shape[1] // num_heads
    query_count = queries.shape[0]
    value_count = pool_keys.shape[0]
    value_blocks = compat.shape[1]
    query_block = query_count // compat.shape[2]
    value_block = value_count // value_blocks
    score_scale = head_width ** (-0.5)
    value_index = lax.axis_index("val")
    offset = value_index * value_count
    block_ids = value_index * value_blocks + jnp.arange(value_blocks, dtype=jnp.int32)
    positions = jnp.arange(value_count, dtype=jnp.int32)

    def head_slices(head_index, first_row):
        col_low = head_index * head_width
        query_tile = queries[first_row : first_row + query_count, col_low : col_low + head_width]
        grad_tile = out_grad[first_row : first_row + query_count, col_low : col_low + head_width]
        return (
            query_tile,
            grad_tile,
            pool_keys[:, col_low : col_low + head_width],
            pool_values[:, col_low : col_low + head_width],
        )

    def first_pass(head_index, first_row, allowed):
        query_tile, grad_tile, key_head, value_head = head_slices(head_index, first_row)
        scores = score_scale * jnp.einsum(
            "qd,kd->qk", query_tile, key_head, preferred_element_type=jnp.float32
        )
        dprobs = jnp.einsum("qd,kd->qk", grad_tile, value_head, preferred_element_type=jnp.float32)
        lse_rows = lse[head_index, first_row : first_row + query_count]
        soft_probs = jnp.where(allowed, jnp.exp(scores - lse_rows[:, None]), 0.0)
        return (soft_probs, dprobs)

    records = []
    for head_index in range(num_heads):
        first_row = 0
        target_ids = targets[first_row : first_row + query_count, head_index]
        block_marks = compat[
            head_index, :, first_row // query_block : (first_row + query_count) // query_block
        ]
        per_query = jnp.broadcast_to(
            jnp.transpose(block_marks)[:, None, :],
            (query_count // query_block, query_block, value_blocks),
        ).reshape(query_count, value_blocks)
        target_hits = (target_ids // value_block)[:, None] == block_ids[None, :]
        usable = (per_query == 1) | target_hits
        layout_allowed = jnp.broadcast_to(
            usable[:, :, None], (query_count, value_blocks, value_block)
        ).reshape(query_count, value_count)
        onehot = ((target_ids - offset)[:, None] == positions[None, :]).astype(jnp.float32)
        allowed, onehot, is_live = (layout_allowed, onehot, jnp.any(usable))
        compute = partial(first_pass, head_index, first_row, allowed)
        outcome = compute()
        records.append((head_index, first_row, allowed, onehot, is_live, outcome))
    local_delta = jnp.stack(
        [
            jnp.concatenate(
                [
                    jnp.sum(record[5][0] * record[5][1], axis=1)
                    for record in records
                    if record[0] == head_index
                ]
            )
            for head_index in range(num_heads)
        ]
    )
    row_delta = lax.psum(local_delta, "val")

    def second_pass(head_index, first_row, soft_probs, dprobs, onehot):
        query_tile, grad_tile, key_head, value_head = head_slices(head_index, first_row)
        delta_rows = row_delta[head_index, first_row : first_row + query_count]
        dscores = soft_probs * (dprobs - delta_rows[:, None] + 1.0) - onehot
        probs_low = soft_probs.astype(jnp.bfloat16)
        dscores_low = dscores.astype(jnp.bfloat16)
        query_term = score_scale * jnp.einsum(
            "qk,kd->qd", dscores_low, key_head, preferred_element_type=jnp.float32
        )
        key_term = score_scale * jnp.einsum(
            "qk,qd->kd", dscores_low, query_tile, preferred_element_type=jnp.float32
        )
        value_term = jnp.einsum(
            "qk,qd->kd", probs_low, grad_tile, preferred_element_type=jnp.float32
        )
        return (query_term, key_term, value_term)

    query_lists = [[] for head_index in range(num_heads)]
    key_sums = [
        jnp.zeros((value_count, head_width), jnp.float32) for head_index in range(num_heads)
    ]
    value_sums = [
        jnp.zeros((value_count, head_width), jnp.float32) for head_index in range(num_heads)
    ]
    for record in records:
        compute = partial(second_pass, record[0], record[1], record[5][0], record[5][1], record[3])
        outcome = compute()
        query_lists[record[0]].append(outcome[0])
        key_sums[record[0]] = outcome[1]
        value_sums[record[0]] = outcome[2]
    query_part = jnp.concatenate([pieces[0] for pieces in query_lists], axis=1)
    pool_part = jnp.concatenate(key_sums + value_sums, axis=1)
    query_grad = lax.psum(query_part, "val").astype(jnp.bfloat16)
    split_width = num_heads * head_width
    pool_whole = lax.psum(pool_part, "qry")
    share_rows = value_count // lax.axis_size("qry")
    pool_grad = lax.dynamic_slice_in_dim(
        pool_whole, lax.axis_index("qry") * share_rows, share_rows, 0
    )
    return (
        query_grad,
        pool_grad[:, :split_width].astype(jnp.bfloat16),
        pool_grad[:, split_width:].astype(jnp.bfloat16),
    )


def solution(mesh):
    placed = (
        P("qry", None),
        P("val", None),
        P("val", None),
        P("qry", None),
        P(None, "qry"),
        P(None, "val", "qry"),
        P("qry", None),
    )
    return jax.shard_map(
        on_device,
        mesh=mesh,
        in_specs=placed,
        out_specs=(P("qry", None), P(("val", "qry"), None), P(("val", "qry"), None)),
        check_vma=False,
    )
```

profile of v0, /device:TPU:1, one launch (start us, length us, event | category | flops | bytes accessed | tf_op | source)
XLA Modules:
  0.0 699.3 jit_solution(14495536286092192248)
XLA Ops:
  0.6 0.7 compare_bitcast_fusion
  1.4 0.9 or_reduce_fusion.1
  2.4 1.9 fusion.16
  4.4 1.0 multiply_reduce_fusion.1
  6.0 0.9 copy-done.8
  7.6 2.7 multiply_reduce_fusion
  10.4 281.7 %psum.21 = f32[2,1536]{1,0:T(2,128)S(1)} all-reduce(f32[2,1536]{1,0:T(2,128)S(1)} %pad_maximum_fusion.2), channel_id=1, replica_groups=mesh['val'=64,'qry'=8] {'val'}, use_global_device_ids=true, to_apply=%region_2.3 | all-reduce | flops 3072 | bytes 24576 | tf_op jit(solution)/shard_map/psum | solution.py:77
  292.2 2.9 subtract_convert_fusion.1
  295.1 0.6 convolution_multiply_fusion.5
  295.8 1.3 copy-done.3
  297.0 0.8 subtract_convert_fusion
  297.9 0.6 convolution_multiply_fusion.4
  298.5 1.3 copy-done.9
  299.9 0.6 fusion.8
  300.5 0.6 fusion.6
  301.1 1.5 pad_maximum_fusion.1
  302.7 63.4 %all-reduce.2 = bf16[512,1024]{0,1:T(8,128)(2,1)S(1)} all-reduce(f32[512,1024]{0,1:T(8,128)} %pad_maximum_fusion.1), channel_id=1, replica_groups=mesh['val'=64,'qry'=8] {'qry'}, use_global_device_ids=true, to_apply=%region_4.5 | all-reduce | flops 524288 | bytes 3145728 | tf_op jit(solution)/shard_map/psum | solution.py:113
  366.2 0.7 copy.11
  367.0 0.7 copy.12
  367.7 1.7 convolution_multiply_fusion.3
  369.4 0.6 convolution_multiply_fusion.2
  370.1 1.9 pad_maximum_fusion
  371.9 325.8 %all-reduce.3 = bf16[1536,512]{0,1:T(8,128)(2,1)S(1)} all-reduce(f32[1536,512]{0,1:T(8,128)} %pad_maximum_fusion), channel_id=1, replica_groups=mesh['val'=64,'qry'=8] {'val'}, use_global_device_ids=true, to_apply=%region_3.4 | all-reduce | flops 786432 | bytes 4718592 | tf_op jit(solution)/shard_map/psum | solution.py:111
  697.7 1.6 copy.10
  (43 shorter events, 1.8 us)
Async XLA Ops:
  2.3 2.0 copy-start.16
  2.3 2.0 copy-start.10
  2.3 2.0 copy-start.12
  4.3 1.7 copy-start
  4.4 2.5 copy-start.8
  4.4 2.6 copy-start.14
  7.6 2.7 copy-start.2
  7.6 284.5 %copy-start.15 = (s32[1536,2]{0,1:T(2,128)S(1)}, s32[1536,2]{0,1:T(2,128)}, u32[]{:S(2)}) copy-start(s32[1536,2]{0,1:T(2,128)} %param.13) | copy-start | bytes 36868
  292.2 2.9 copy-start.13
  292.2 3.6 copy-start.1
  292.2 4.8 copy-start.3
  295.1 2.7 copy-start.4
  297.9 2.6 copy-start.6
  297.9 2.0 copy-start.9
  302.7 65.0 %copy-start.5 = (bf16[1536,512]{0,1:T(8,128)(2,1)S(1)}, bf16[1536,512]{0,1:T(8,128)(2,1)}, u32[]{:S(2)}) copy-start(bf16[1536,512]{0,1:T(8,128)(2,1)} %copy-done.4) | copy-start | bytes 4718596
  367.7 1.7 copy-start.7
  367.7 1.7 copy-start.11
where the time goes:
time: 710 us; the launch traced here: 699 us
  blocking collectives  671 us (95%)
  matrix products  11.1 us (2%)
  other arithmetic  8.76 us (1%)
  local copies, waits for them, and re-layouts  7.58 us (1%)
    psum x1, blocking collectives, on_device(): query_grad = lax.psum(query_part, 'val').astype(jnp.bfloat16)  326 us
    psum x1, blocking collectives, on_device(): row_delta = lax.psum(local_delta, 'val')  282 us
    psum x1, blocking collectives, on_device(): pool_whole = lax.psum(pool_part, 'qry')  63.4 us

commit v1 on v0

--- a/solution.py
+++ b/solution.py
@@ -3,7 +3,221 @@
 import jax
 import jax.numpy as jnp
 from jax import lax
+from jax.experimental import pallas as pl
+from jax.experimental.pallas import tpu as pltpu
 from jax.sharding import PartitionSpec as P
+
+ZH, Y, CORES, ZL, X = 4, 8, 2, 2, 4
+MESH = pl.DeviceIdType.MESH
+VMEM = pl.BlockSpec(memory_space=pltpu.VMEM)
+
+
+def place():
+    val, qry = lax.axis_index("val"), lax.axis_index("qry")
+    core, y, zh = val % CORES, (val // CORES) % Y, val // (CORES * Y)
+    return core, y, zh, qry // X, qry % X
+
+
+def device(core, y, zh, zl, x):
+    return ((zh * Y + y) * CORES + core, zl * X + x)
+
+
+def neighbours():
+    core, y, zh, zl, x = place()
+    across = device(1 - core, y, zh, zl, x)
+    along_y = [device(core, (y + d) % Y, zh, zl, x) for d in range(1, Y)]
+    along_z = [device(core, y, (zh + d) % ZH, zl, x) for d in range(1, ZH)]
+    along_x = [device(core, y, zh, zl, (x + d) % X) for d in range(1, X)]
+    beside = device(core, y, zh, 1 - zl, x)
+    return across, along_y, along_z, along_x, beside
+
+
+def greet(devices):
+    barrier = pltpu.get_barrier_semaphore()
+    for there in devices:
+        pl.semaphore_signal(barrier, inc=1, device_id=there, device_id_type=MESH)
+    pl.semaphore_wait(barrier, len(devices))
+
+
+def push(src, dst, send, recv, there):
+    copy = pltpu.make_async_remote_copy(
+        src_ref=src, dst_ref=dst, send_sem=send, recv_sem=recv, device_id=there, device_id_type=MESH
+    )
+    copy.start()
+    return copy
+
+
+def delta_kernel(part, total, from_core, sum_core, from_y, sum_y, from_z, send, recv):
+    across, along_y, along_z, _, _ = neighbours()
+    greet([across] + along_y + along_z)
+    copies = [push(part, from_core, send.at[0], recv.at[0], across)]
+    copies[0].wait_recv()
+    sum_core[...] = part[...] + from_core[...]
+    stage = [
+        push(sum_core, from_y.at[d], send.at[1 + d], recv.at[1 + d], there)
+        for d, there in enumerate(along_y)
+    ]
+    acc = sum_core[...]
+    for d, copy in enumerate(stage):
+        copy.wait_recv()
+        acc = acc + from_y[d]
+    sum_y[...] = acc
+    copies += stage
+    stage = [
+        push(sum_y, from_z.at[d], send.at[Y + d], recv.at[Y + d], there)
+        for d, there in enumerate(along_z)
+    ]
+    for d, copy in enumerate(stage):
+        copy.wait_recv()
+        acc = acc + from_z[d]
+    total[...] = acc
+    for copy in copies + stage:
+        copy.wait_send()
+
+
+def sum_delta(part):
+    shape = part.shape
+    flat = part.reshape(-1, 128)
+    rows = flat.shape
+    f32 = jnp.float32
+    return pl.pallas_call(
+        delta_kernel,
+        out_shape=jax.ShapeDtypeStruct(rows, f32),
+        in_specs=[VMEM],
+        out_specs=VMEM,
+        scratch_shapes=[
+            pltpu.VMEM(rows, f32),
+            pltpu.VMEM(rows, f32),
+            pltpu.VMEM((Y - 1, *rows), f32),
+            pltpu.VMEM(rows, f32),
+            pltpu.VMEM((ZH - 1, *rows), f32),
+            pltpu.SemaphoreType.DMA((Y + ZH - 1,)),
+            pltpu.SemaphoreType.DMA((Y + ZH - 1,)),
+        ],
+        compiler_params=pltpu.CompilerParams(collective_id=0, has_side_effects=True),
+    )(flat).reshape(shape)
+
+
+def grads_kernel(
+    query, pool, query_out, key_out, value_out,
+    from_core, sum_core, from_y, sum_y, from_z, mine, line,
+    from_x, sum_x, from_beside, send, recv,
+):
+    f32, low = jnp.float32, jnp.bfloat16
+    core, y, zh, zl, x = place()
+    across, along_y, along_z, along_x, beside = neighbours()
+    greet([across] + along_y + along_z + along_x + [beside])
+    half = from_core.shape[0]
+    piece = half // Y
+    width = query.shape[1] // ZH
+    done = []
+    used = iter(range(send.shape[0]))
+
+    def start(src, dst, there):
+        n = next(used)
+        copy = push(src, dst, send.at[n], recv.at[n], there)
+        done.append(copy)
+        return copy
+
+    far = pl.multiple_of((1 - core) * half, half)
+    near = pl.multiple_of(core * half, half)
+    swap = start(query.at[pl.ds(far, half)], from_core, across)
+    x_stage = [
+        start(pool.at[:, (x + d) % X], from_x.at[d - 1], there)
+        for d, there in zip(range(1, X), along_x)
+    ]
+    swap.wait_recv()
+    sum_core[...] = (query[pl.ds(near, half), :].astype(f32) + from_core[...].astype(f32)).astype(low)
+    y_stage = [
+        start(
+            sum_core.at[pl.ds(pl.multiple_of((y + d) % Y * piece, piece), piece)],
+            from_y.at[d - 1],
+            there,
+        )
+        for d, there in zip(range(1, Y), along_y)
+    ]
+    acc = pool[:, x].astype(f32)
+    for d, copy in enumerate(x_stage):
+        copy.wait_recv()
+        acc = acc + from_x[d].astype(f32)
+    sum_x[...] = acc.astype(low)
+    zl_copy = start(sum_x.at[1 - zl], from_beside, beside)
+    acc = sum_core[pl.ds(pl.multiple_of(y * piece, piece), piece), :].astype(f32)
+    for d, copy in enumerate(y_stage):
+        copy.wait_recv()
+        acc = acc + from_y[d].astype(f32)
+    sum_y[...] = acc.astype(low)
+    z_stage = [
+        start(
+            sum_y.at[:, pl.ds(pl.multiple_of((zh + d) % ZH * width, width), width)],
+            from_z.at[d - 1],
+            there,
+        )
+        for d, there in zip(range(1, ZH), along_z)
+    ]
+    zl_copy.wait_recv()
+    pool_sum = (sum_x[zl].astype(f32) + from_beside[...].astype(f32)).astype(low)
+    split = pool_sum.shape[1] // 2
+    key_out[...] = pool_sum[:, :split]
+    value_out[...] = pool_sum[:, split:]
+    own_columns = pl.ds(pl.multiple_of(zh * width, width), width)
+    acc = sum_y[:, own_columns].astype(f32)
+    for d, copy in enumerate(z_stage):
+        copy.wait_recv()
+        acc = acc + from_z[d].astype(f32)
+    mine[...] = acc.astype(low)
+    back_z = [start(mine, line.at[:, own_columns], there) for there in along_z]
+    line[:, own_columns] = mine[...]
+    for copy in back_z:
+        copy.wait_recv()
+    own_rows = pl.ds(pl.multiple_of(core * half + y * piece, piece), piece)
+    back_y = [start(line, query_out.at[own_rows], there) for there in along_y]
+    query_out[own_rows, :] = line[...]
+    back_core = [start(line, query_out.at[own_rows], across)]
+    for d, copy in zip(range(1, Y), back_y):
+        copy.wait_recv()
+        rows = pl.ds(pl.multiple_of(core * half + (y + Y - d) % Y * piece, piece), piece)
+        back_core.append(start(query_out.at[rows], query_out.at[rows], across))
+    for copy in back_core:
+        copy.wait_recv()
+    for copy in done:
+        copy.wait_send()
+
+
+def sum_grads(query, pool):
+    low = jnp.bfloat16
+    count, columns = query.shape
+    rows, wide = pool.shape
+    share = rows // (ZL * X)
+    half = count // CORES
+    piece = half // Y
+    width = columns // ZH
+    copies = 1 + (X - 1) + (Y - 1) + 1 + (ZH - 1) * 2 + (Y - 1) + Y
+    return pl.pallas_call(
+        grads_kernel,
+        out_shape=(
+            jax.ShapeDtypeStruct(query.shape, low),
+            jax.ShapeDtypeStruct((share, wide // 2), low),
+            jax.ShapeDtypeStruct((share, wide // 2), low),
+        ),
+        in_specs=[VMEM, VMEM],
+        out_specs=(VMEM, VMEM, VMEM),
+        scratch_shapes=[
+            pltpu.VMEM((half, columns), low),
+            pltpu.VMEM((half, columns), low),
+            pltpu.VMEM((Y - 1, piece, columns), low),
+            pltpu.VMEM((piece, columns), low),
+            pltpu.VMEM((ZH - 1, piece, width), low),
+            pltpu.VMEM((piece, width), low),
+            pltpu.VMEM((piece, columns), low),
+            pltpu.VMEM((X - 1, ZL, share, wide), low),
+            pltpu.VMEM((ZL, share, wide), low),
+            pltpu.VMEM((share, wide), low),
+            pltpu.SemaphoreType.DMA((copies,)),
+            pltpu.SemaphoreType.DMA((copies,)),
+        ],
+        compiler_params=pltpu.CompilerParams(collective_id=1, has_side_effects=True),
+    )(query, pool.reshape(ZL, X, share, wide))
 
 
 def on_device(queries, pool_keys, pool_values, out_grad, lse, compat, targets):
@@ -74,7 +288,7 @@
             for head_index in range(num_heads)
         ]
     )
-    row_delta = lax.psum(local_delta, "val")
+    row_delta = sum_delta(local_delta)
 
     def second_pass(head_index, first_row, soft_probs, dprobs, onehot):
         query_tile, grad_tile, key_head, value_head = head_slices(head_index, first_row)
@@ -108,18 +322,7 @@
         value_sums[record[0]] = outcome[2]
     query_part = jnp.concatenate([pieces[0] for pieces in query_lists], axis=1)
     pool_part = jnp.concatenate(key_sums + value_sums, axis=1)
-    query_grad = lax.psum(query_part, "val").astype(jnp.bfloat16)
-    split_width = num_heads * head_width
-    pool_whole = lax.psum(pool_part, "qry")
-    share_rows = value_count // lax.axis_size("qry")
-    pool_grad = lax.dynamic_slice_in_dim(
-        pool_whole, lax.axis_index("qry") * share_rows, share_rows, 0
-    )
-    return (
-        query_grad,
-        pool_grad[:, :split_width].astype(jnp.bfloat16),
-        pool_grad[:, split_width:].astype(jnp.bfloat16),
-    )
+    return sum_grads(query_part.astype(jnp.bfloat16), pool_part.astype(jnp.bfloat16))
 
 
 def solution(mesh):

time: 710 us -> 117 us (0.16); the launches traced: 699 us -> 117 us
  blocking collectives: 671 us -> 0 us
  Pallas kernels: 0 us -> 89 us
    psum x3 -> x0, blocking collectives: 671 us -> none  [the longest x1 326 us: on_device(): query_grad = lax.psum(query_part, 'val').astype(jnp.bfloat16)]
    pallas_call x0 -> x2, Pallas kernels: none -> 89 us  [the longest x1 63.7 us: sum_grads(): pl.pallas_call(grads_kernel, out_shape=(jax.ShapeDtypeStruct(query.shape,...]
where the time goes in v1:
time: 117 us
  Pallas kernels  89 us (76%)
  matrix products  9.8 us (8%)
  local copies, waits for them, and re-layouts  9.31 us (8%)
  other arithmetic  7.74 us (7%)
    pallas_call x1, Pallas kernels, sum_grads(): pl.pallas_call(grads_kernel, out_shape=(jax.ShapeDtypeStruct(query.shape,...  63.7 us
    pallas_call x1, Pallas kernels, sum_delta(): pl.pallas_call(delta_kernel, out_shape=jax.ShapeDtypeStruct(rows, f32), i...  25.3 us
    unnamed x36, local copies, waits for them, and re-layouts  7.87 us
    convert_element_type x2, other arithmetic, second_pass(): dscores_low = dscores.astype(jnp.bfloat16)  3.74 us
    dot_general x2, matrix products, first_pass(): jnp.einsum('qd,kd->qk', query_tile, key_head, preferred_element_type=jnp....  3.69 us
    dot_general x2, matrix products, first_pass(): jnp.einsum('qd,kd->qk', grad_tile, value_head, preferred_element_type=jnp...  2.54 us

profile of v1, /device:TPU:1, one launch (start us, length us, event | category | flops | bytes accessed | tf_op | source)
XLA Modules:
  0.0 116.8 jit_solution(10902119929668897487)
XLA Ops:
  0.6 0.7 compare_bitcast_fusion
  1.4 0.9 or_reduce_fusion.1
  2.4 1.9 %fusion.26 = f32[1536,512]{0,1:T(8,128)S(1)} fusion(bf16[1536,512]{1,0:T(8,128)(2,1)} %param.10, bf16[512,512]{1,0:T(8,128)(2,1)} %param.9), kind=kOutput, calls=%fused_computation.36 | convolution fusion | flops 402653184 | bytes 4194304 | tf_op jit(solution)/shard_map/qd,kd->qk/dot_general | solution.py:253
  4.4 1.0 multiply_reduce_fusion.1
  6.0 0.9 copy-done.4
  7.0 0.6 fusion.21
  7.6 2.7 %multiply_reduce_fusion = (f32[1536]{0:T(1024)S(1)}, f32[1536,512]{0,1:T(8,128)}) fusion(f32[1536,512]{0,1:T(8,128)S(1)} %fusion.21, f32[1536]{0:T(1024)S(1)} %get-tuple-element.8, bf16[512,512]{1,0:T(8,128)(2,1)S(1)} %copy-done.9, bf16[1536,512]{1,0:T(8,128)(2,1)S(1)} %copy-done.6, pred[1536]{0:T(1024)(128)(4,1)S(1)} %get-tuple-element.6), kind=kOutput, calls=%fused_computation.12 | convolution fusion | flops 406583808 | bytes 7356416 | tf_op jit(solution)/shard_map/qd,kd->qk/dot_general | solution.py:250
  10.3 0.6 reshape.94.part
  10.9 25.3 %shard_map.94 = f32[24,128]{1,0:T(8,128)} custom-call(f32[24,128]{1,0:T(8,128)} %reshape.94.part), custom_call_target="tpu_custom_call" | custom-call | tf_op jit(solution)/shard_map/pallas_call | solution.py:83
  36.2 0.8 slice_bitcast_fusion.1
  37.1 2.9 %subtract_convert_fusion.1 = bf16[1536,512]{0,1:T(8,128)(2,1)S(1)} fusion(f32[1536,512]{0,1:T(8,128)S(1)} %get-tuple-element.16, f32[1536,512]{0,1:T(8,128)} %copy-done, s32[1536]{0:T(1024)S(1)} %get-tuple-element.3, f32[1536]{0:T(1024)S(1)} %get-tuple-element.9), kind=kLoop, calls=%fused_computation.10 | loop fusion | flops 5505024 | bytes 7876608 | tf_op jit(solution)/shard_map/convert_element_type | solution.py:298
  40.6 1.4 %copy-done.1 = f32[1536,512]{0,1:T(8,128)S(1)} copy-done((f32[1536,512]{0,1:T(8,128)S(1)}, f32[1536,512]{0,1:T(8,128)}, u32[]{:S(2)}) %copy-start.1) | copy-done | bytes 3145752
  42.0 0.8 subtract_convert_fusion
  43.4 0.8 copy-done.5
  44.2 0.6 fusion.12
  44.8 0.6 fusion.15
  45.5 1.1 pad_maximum_fusion.1.pool
  46.6 0.6 fusion.6
  47.2 0.6 fusion.7
  47.8 1.3 %pad_maximum_fusion.query = bf16[1536,512]{1,0:T(8,128)(2,1)} fusion(bf16[1536,256]{1,0:T(8,128)(2,1)S(1)} %fusion.7, bf16[1536,256]{1,0:T(8,128)(2,1)S(1)} %fusion.6), kind=kLoop, calls=%fused_computation.18 | loop fusion | flops 3145728 | bytes 3145728 | tf_op jit(solution)/shard_map/concatenate | solution.py:323
  49.1 63.7 %shard_map.95 = (bf16[1536,512]{1,0:T(8,128)(2,1)}, bf16[64,512]{1,0:T(8,128)(2,1)}, bf16[64,512]{1,0:T(8,128)(2,1)}) custom-call(bf16[1536,512]{1,0:T(8,128)(2,1)} %pad_maximum_fusion.query, bf16[2,4,64,1024]{3,2,1,0:T(8,128)(2,1)} %pad_maximum_fusion.1.pool), custom_call_target="tpu_custom_call" | custom-call | tf_op jit(solution)/shard_map/pallas_call | solution.py:196
  112.8 2.7 %copy.19 = bf16[1536,512]{1,0:T(8,128)(2,1)} copy(bf16[1536,512]{1,0:T(8,128)(2,1)} %get-tuple-element.22) | data formatting | bytes 3145728
  115.5 0.6 copy.20
  116.1 0.6 copy.21
  (37 shorter events, 2.1 us)
Async XLA Ops:
  2.3 2.0 %copy-start.14 = (f32[2,1536]{1,0:T(2,128)S(1)}, f32[2,1536]{1,0:T(2,128)}, u32[]{:S(2)}) copy-start(f32[2,1536]{1,0:T(2,128)} %param.11) | copy-start | bytes 36868
  2.3 2.0 %copy-start.6 = (bf16[1536,512]{1,0:T(8,128)(2,1)S(1)}, bf16[1536,512]{1,0:T(8,128)(2,1)}, u32[]{:S(2)}) copy-start(bf16[1536,512]{1,0:T(8,128)(2,1)} %param.7) | copy-start | bytes 4718596
  2.3 2.0 %copy-start.9 = (bf16[512,512]{1,0:T(8,128)(2,1)S(1)}, bf16[512,512]{1,0:T(8,128)(2,1)}, u32[]{:S(2)}) copy-start(bf16[512,512]{1,0:T(8,128)(2,1)} %param.8) | copy-start | bytes 1572868
  4.3 1.7 %copy-start = (f32[1536,512]{0,1:T(8,128)}, f32[1536,512]{0,1:T(8,128)S(1)}, u32[]{:S(2)}) copy-start(f32[1536,512]{0,1:T(8,128)S(1)} %fusion.26) | copy-start | bytes 9437188
  4.4 2.5 %copy-start.4 = (bf16[1536,512]{1,0:T(8,128)(2,1)S(1)}, bf16[1536,512]{1,0:T(8,128)(2,1)}, u32[]{:S(2)}) copy-start(bf16[1536,512]{1,0:T(8,128)(2,1)} %param.10) | copy-start | bytes 4718596
  4.4 2.6 %copy-start.8 = (bf16[512,512]{1,0:T(8,128)(2,1)S(1)}, bf16[512,512]{1,0:T(8,128)(2,1)}, u32[]{:S(2)}) copy-start(bf16[512,512]{1,0:T(8,128)(2,1)} %param.9) | copy-start | bytes 1572868
  7.6 2.7 %copy-start.2 = (f32[1536,512]{0,1:T(8,128)}, f32[1536,512]{0,1:T(8,128)S(1)}, u32[]{:S(2)}) copy-start(f32[1536,512]{0,1:T(8,128)S(1)} %fusion.21) | copy-start | bytes 9437188
  7.6 29.4 %copy-start.13 = (s32[1536,2]{0,1:T(2,128)S(1)}, s32[1536,2]{0,1:T(2,128)}, u32[]{:S(2)}) copy-start(s32[1536,2]{0,1:T(2,128)} %param.13) | copy-start | bytes 36868
  37.1 2.9 %copy-start.7 = (bf16[1536,512]{1,0:T(8,128)(2,1)S(1)}, bf16[1536,512]{1,0:T(8,128)(2,1)}, u32[]{:S(2)}) copy-start(bf16[1536,512]{1,0:T(8,128)(2,1)} %param.7) | copy-start | bytes 4718596
  37.1 3.5 %copy-start.3 = (f32[1536,512]{0,1:T(8,128)S(1)}, f32[1536,512]{0,1:T(8,128)}, u32[]{:S(2)}) copy-start(f32[1536,512]{0,1:T(8,128)} %copy-done.2) | copy-start | bytes 9437188
  40.0 2.0 %copy-start.1 = (f32[1536,512]{0,1:T(8,128)S(1)}, f32[1536,512]{0,1:T(8,128)}, u32[]{:S(2)}) copy-start(f32[1536,512]{0,1:T(8,128)} %get-tuple-element.14) | copy-start | bytes 9437188
  42.8 1.4 %copy-start.5 = (bf16[1536,512]{1,0:T(8,128)(2,1)S(1)}, bf16[1536,512]{1,0:T(8,128)(2,1)}, u32[]{:S(2)}) copy-start(bf16[1536,512]{1,0:T(8,128)(2,1)} %param.10) | copy-start | bytes 4718596
  45.4 1.1 copy-start.10
  112.8 2.7 %copy-start.12 = (bf16[64,512]{1,0:T(8,128)(2,1)S(1)}, bf16[64,512]{1,0:T(8,128)(2,1)}, u32[]{:S(2)}) copy-start(bf16[64,512]{1,0:T(8,128)(2,1)} %get-tuple-element.23) | copy-start | bytes 196612
  112.8 3.3 %copy-start.11 = (bf16[64,512]{1,0:T(8,128)(2,1)S(1)}, bf16[64,512]{1,0:T(8,128)(2,1)}, u32[]{:S(2)}) copy-start(bf16[64,512]{1,0:T(8,128)(2,1)} %get-tuple-element.24) | copy-start | bytes 196612

commit v2 on v0

v2 whole, which is shorter than its diff:
```python
import jax
import jax.numpy as jnp
from jax import lax
from jax.experimental import pallas as pl
from jax.experimental.pallas import tpu as pltpu
from jax.sharding import PartitionSpec as P

ZH, Y, CORES, ZL, X = 4, 8, 2, 2, 4
UP, DOWN = 4, 3
CHUNKS, POOL_WAIT = 2, 4
MESH = pl.DeviceIdType.MESH
VMEM = pl.BlockSpec(memory_space=pltpu.VMEM)


def place():
    val, qry = lax.axis_index("val"), lax.axis_index("qry")
    core, y, zh = val % CORES, (val // CORES) % Y, val // (CORES * Y)
    return core, y, zh, qry // X, qry % X


def device(core, y, zh, zl, x):
    return ((zh * Y + y) * CORES + core, zl * X + x)


def neighbours():
    core, y, zh, zl, x = place()
    across = device(1 - core, y, zh, zl, x)
    along_y = [device(core, (y + d) % Y, zh, zl, x) for d in range(1, Y)]
    along_z = [device(core, y, (zh + d) % ZH, zl, x) for d in range(1, ZH)]
    along_x = [device(core, y, zh, zl, (x + d) % X) for d in range(1, X)]
    beside = device(core, y, zh, 1 - zl, x)
    return across, along_y, along_z, along_x, beside


def mult(first, size):
    return pl.ds(pl.multiple_of(first, size), size)


def dot(a, b, dims):
    return lax.dot_general(a, b, ((dims[:1], dims[1:]), ((), ())), preferred_element_type=jnp.float32)


def push(src, dst, send, recv, there):
    copy = pltpu.make_async_remote_copy(
        src_ref=src, dst_ref=dst, send_sem=send, recv_sem=recv, device_id=there, device_id_type=MESH
    )
    copy.start()
    return copy


def backward_kernel(
    queries, grads, keys, values, lse, local, query_out, key_out, value_out,
    probs, weights, delta, delta_core, delta_sum, delta_y, delta_line, delta_z, query, sums, key_sums, pool,
    from_core, up_in, down_in, up_out, down_out, sum_y, from_z, mine, line,
    from_x, sum_x, from_beside, send, recv,
):
    f32, low = jnp.float32, jnp.bfloat16
    core, y, zh, zl, x = place()
    across, along_y, along_z, along_x, beside = neighbours()
    upper, lower = along_y[0], along_y[-1]
    friends = [across] + along_y + along_z + along_x + [beside]
    barrier = pltpu.get_barrier_semaphore()
    for there in friends:
        pl.semaphore_signal(barrier, inc=1, device_id=there, device_id_type=MESH)

    count, columns = queries.shape
    tiles, tile = lse.shape
    heads = probs.shape[0]
    head_width = columns // heads
    per_head = tiles // heads
    scale = head_width ** (-0.5)
    half = from_core.shape[1]
    piece = half // Y
    width = columns // ZH
    share = key_out.shape[0]
    own_columns = mult(zh * width, width)
    done = []
    used = iter(range(send.shape[0]))

    def start(src, dst, there):
        n = next(used)
        copy = push(src, dst, send.at[n], recv.at[n], there)
        done.append(copy)
        return copy

    def head_columns(h):
        return pl.ds(h * head_width, head_width)

    for h in range(heads):
        cols = head_columns(h)
        sums[...] = jnp.zeros_like(sums)

        def first_pass(b, carry):
            rows = mult(b * tile, tile)
            grad_tile = grads[rows, cols]
            scores = dot(keys[:, cols], queries[rows, cols], (1, 1)) * scale
            p = jnp.exp(scores - lse[pl.ds(h * per_head + b, 1), :])
            dprobs = dot(values[:, cols], grad_tile, (1, 1))
            terms = p * dprobs
            delta[pl.ds(h * per_head + b, 1), :] = jnp.sum(terms, axis=0, keepdims=True)
            slot = lax.broadcasted_iota(jnp.int32, p.shape, 0)
            hit = slot == local[pl.ds(h * per_head + b, 1), :]
            probs[h, :, rows] = p
            weights[h, :, rows] = terms + p - jnp.where(hit, 1.0, 0.0)
            sums[...] += dot(p.astype(low), grad_tile, (1, 0))
            return carry

        lax.fori_loop(0, per_head, first_pass, 0)
        for r in range(ZL * X):
            pool[1, r // X, r % X, :, cols] = sums[pl.ds(r * share, share), :].astype(low)

    pl.semaphore_wait(barrier, len(friends))

    def pool_steps(n, out, wait):
        x_stage = [
            start(pool.at[n, :, (x + d) % X], from_x.at[n, d - 1], there)
            for d, there in zip(range(1, X), along_x)
        ]
        for _ in range(wait):
            yield
        acc = pool[n, :, x].astype(f32)
        for d, copy in enumerate(x_stage):
            copy.wait_recv()
            acc = acc + from_x[n, d].astype(f32)
        sum_x[n] = acc.astype(low)
        copy = start(sum_x.at[n, 1 - zl], from_beside.at[n], beside)
        for _ in range(3):
            yield
        copy.wait_recv()
        out[...] = (sum_x[n, zl].astype(f32) + from_beside[n].astype(f32)).astype(low)

    swap = start(delta, delta_core, across)
    swap.wait_recv()
    delta_sum[...] = delta[...] + delta_core[...]
    stage = [start(delta_sum, delta_y.at[d], there) for d, there in enumerate(along_y)]
    value_lane = pool_steps(1, value_out, 1)
    next(value_lane)
    acc = delta_sum[...]
    for d, copy in enumerate(stage):
        copy.wait_recv()
        acc = acc + delta_y[d]
    delta_line[...] = acc
    stage = [start(delta_line, delta_z.at[d], there) for d, there in enumerate(along_z)]
    for d, copy in enumerate(stage):
        copy.wait_recv()
        acc = acc + delta_z[d]
    delta_core[...] = acc

    def rows(k, c, owner):
        first = k * CORES * half + c * half + lax.rem(owner + Y, Y) * piece
        return pl.ds(pl.multiple_of(first, piece), piece)

    def half_rows(k, c):
        return pl.ds(pl.multiple_of(k * CORES * half + c * half, half), half)

    def own(k, owner):
        inside = pl.ds(pl.multiple_of(lax.rem(owner + Y, Y) * piece, piece), piece)
        return query[rows(k, core, owner), :].astype(f32) + from_core[k, inside, :].astype(f32)

    def query_steps(k):
        swap = start(query.at[half_rows(k, 1 - core)], from_core.at[k], across)
        yield
        swap.wait_recv()
        up_out[k, 0] = own(k, y + UP).astype(low)
        up = start(up_out.at[k, 0], up_in.at[k, 0], upper)
        down_out[k, 0] = own(k, y - DOWN).astype(low)
        down = start(down_out.at[k, 0], down_in.at[k, 0], lower)
        for s in range(1, UP):
            yield
            up.wait_recv()
            up_out[k, s] = (own(k, y + UP - s) + up_in[k, s - 1].astype(f32)).astype(low)
            up = start(up_out.at[k, s], up_in.at[k, s], upper)
            if s < DOWN:
                down.wait_recv()
                down_out[k, s] = (own(k, y - DOWN + s) + down_in[k, s - 1].astype(f32)).astype(low)
                down = start(down_out.at[k, s], down_in.at[k, s], lower)
        yield
        down.wait_recv()
        up.wait_recv()
        total = own(k, y) + up_in[k, UP - 1].astype(f32) + down_in[k, DOWN - 1].astype(f32)
        sum_y[k] = total.astype(low)
        z_stage = [
            start(
                sum_y.at[k, :, pl.ds(pl.multiple_of((zh + d) % ZH * width, width), width)],
                from_z.at[k, d - 1],
                there,
            )
            for d, there in zip(range(1, ZH), along_z)
        ]
        yield
        acc = sum_y[k, :, own_columns].astype(f32)
        for d, copy in enumerate(z_stage):
            copy.wait_recv()
            acc = acc + from_z[k, d].astype(f32)
        mine[k] = acc.astype(low)
        back_z = [start(mine.at[k], line.at[k, :, own_columns], there) for there in along_z]
        line[k, :, own_columns] = mine[k]
        yield
        for copy in back_z:
            copy.wait_recv()
        here = rows(k, core, y)
        up = start(line.at[k], query_out.at[here], upper)
        down = start(line.at[k], query_out.at[here], lower)
        query_out[here, :] = line[k]
        back_core = [start(line.at[k], query_out.at[here], across)]
        for s in range(1, UP + 1):
            yield
            up.wait_recv()
            got = query_out.at[rows(k, core, y - s)]
            if s < UP:
                up = start(got, got, upper)
            forward = [got]
            if s <= DOWN:
                down.wait_recv()
                got = query_out.at[rows(k, core, y + s)]
                if s < DOWN:
                    down = start(got, got, lower)
                forward.append(got)
            back_core += [start(got, got, across) for got in forward]
        yield
        for copy in back_core:
            copy.wait_recv()

    def second_pass(k, h):
        cols = head_columns(h)

        def step(b, carry):
            rows = mult(b * tile, tile)
            d = delta_core[pl.ds(h * per_head + b, 1), :]
            dscores = (weights[h, :, rows] - probs[h, :, rows] * d).astype(low)
            query[rows, cols] = (dot(dscores, keys[:, cols], (0, 0)) * scale).astype(low)
            key_sums[:, cols] += dot(dscores, queries[rows, cols], (1, 0))
            return carry

        per_chunk = per_head // CHUNKS
        lax.fori_loop(k * per_chunk, (k + 1) * per_chunk, step, 0)

    key_sums[...] = jnp.zeros_like(key_sums)
    lanes = [value_lane]
    for k in range(CHUNKS):
        for h in range(heads):
            second_pass(k, h)
        lanes.append(query_steps(k))
        next(lanes[-1])
    for r in range(ZL * X):
        pool[0, r // X, r % X] = (key_sums[pl.ds(r * share, share), :] * scale).astype(low)
    lanes.append(pool_steps(0, key_out, POOL_WAIT))
    while lanes:
        lanes = [steps for steps in lanes if next(steps, lanes) is not lanes]
    for copy in done:
        copy.wait_send()


def on_device(queries, pool_keys, pool_values, out_grad, lse, compat, targets):
    heads, value_blocks, query_blocks = compat.shape
    count, columns = queries.shape
    value_count = pool_keys.shape[0]
    val = lax.axis_index("val")
    query_block = count // query_blocks
    tiles = heads * query_blocks
    low, f32 = jnp.bfloat16, jnp.float32
    wanted = jnp.transpose(targets)
    marks = jnp.repeat(compat[:, 0, :], query_block, axis=1)
    usable = (marks == 1) | (wanted // value_count == val)
    lse_rows = jnp.where(usable, lse, 3e38).reshape(tiles, query_block)
    local = (wanted - val * value_count).reshape(tiles, query_block)
    share = value_count // (ZL * X)
    half = count // (CORES * CHUNKS)
    piece = half // Y
    width = columns // ZH
    copies = CHUNKS * (1 + (Y - 1) + (ZH - 1) * 2 + (Y - 1) + Y) + 2 * X + 1 + (Y - 1) + (ZH - 1)
    row = (tiles, query_block)
    return pl.pallas_call(
        backward_kernel,
        out_shape=(
            jax.ShapeDtypeStruct(queries.shape, low),
            jax.ShapeDtypeStruct((share, columns), low),
            jax.ShapeDtypeStruct((share, columns), low),
        ),
        in_specs=[VMEM] * 6,
        out_specs=(VMEM, VMEM, VMEM),
        scratch_shapes=[
            pltpu.VMEM((heads, value_count, count), f32),
            pltpu.VMEM((heads, value_count, count), f32),
            pltpu.VMEM(row, f32),
            pltpu.VMEM(row, f32),
            pltpu.VMEM(row, f32),
            pltpu.VMEM((Y - 1, *row), f32),
            pltpu.VMEM(row, f32),
            pltpu.VMEM((ZH - 1, *row), f32),
            pltpu.VMEM(queries.shape, low),
            pltpu.VMEM((value_count, columns // heads), f32),
            pltpu.VMEM((value_count, columns), f32),
            pltpu.VMEM((2, ZL, X, share, columns), low),
            pltpu.VMEM((CHUNKS, half, columns), low),
            pltpu.VMEM((CHUNKS, UP, piece, columns), low),
            pltpu.VMEM((CHUNKS, DOWN, piece, columns), low),
            pltpu.VMEM((CHUNKS, UP, piece, columns), low),
            pltpu.VMEM((CHUNKS, DOWN, piece, columns), low),
            pltpu.VMEM((CHUNKS, piece, columns), low),
            pltpu.VMEM((CHUNKS, ZH - 1, piece, width), low),
            pltpu.VMEM((CHUNKS, piece, width), low),
            pltpu.VMEM((CHUNKS, piece, columns), low),
            pltpu.VMEM((2, X - 1, ZL, share, columns), low),
            pltpu.VMEM((2, ZL, share, columns), low),
            pltpu.VMEM((2, share, columns), low),
            pltpu.SemaphoreType.DMA((copies,)),
            pltpu.SemaphoreType.DMA((copies,)),
        ],
        compiler_params=pltpu.CompilerParams(
            collective_id=0, has_side_effects=True, vmem_limit_bytes=56 * 1024 * 1024
        ),
    )(queries, out_grad, pool_keys, pool_values, lse_rows, local)


def solution(mesh):
    placed = (
        P("qry", None),
        P("val", None),
        P("val", None),
        P("qry", None),
        P(None, "qry"),
        P(None, "val", "qry"),
        P("qry", None),
    )
    return jax.shard_map(
        on_device,
        mesh=mesh,
        in_specs=placed,
        out_specs=(P("qry", None), P(("val", "qry"), None), P(("val", "qry"), None)),
        check_vma=False,
    )
```

time: 710 us -> 86.5 us (0.12); the launches traced: 699 us -> 86.2 us
  blocking collectives: 671 us -> 0 us
  Pallas kernels: 0 us -> 78.1 us
  matrix products: 11.1 us -> 0 us
    psum x3 -> x0, blocking collectives: 671 us -> none  [the longest x1 326 us: on_device(): query_grad = lax.psum(query_part, 'val').astype(jnp.bfloat16)]
    pallas_call x0 -> x1, Pallas kernels: none -> 78.1 us  [on_device(): pl.pallas_call(backward_kernel, out_shape=(jax.ShapeDtypeStruct(queries.s...]
    dot_general x10 -> x0, matrix products: 11.1 us -> none  [the longest x2 3.73 us: first_pass(): jnp.einsum('qd,kd->qk', query_tile, key_head, preferred_element_type=jnp....]
where the time goes in v2:
time: 86.5 us; the launch traced here: 86.2 us
  Pallas kernels  78.1 us (90%)
  local copies, waits for them, and re-layouts  5.29 us (6%)
  other arithmetic  2.17 us (3%)
    pallas_call x1, Pallas kernels, on_device(): pl.pallas_call(backward_kernel, out_shape=(jax.ShapeDtypeStruct(queries.s...  78.1 us
    unnamed x10, local copies, waits for them, and re-layouts  4.05 us

profile of v2, /device:TPU:1, one launch (start us, length us, event | category | flops | bytes accessed | tf_op | source)
XLA Modules:
  0.0 86.2 jit_solution(16969295765808128751)
XLA Ops:
  0.6 0.7 broadcast_compare_fusion
  1.3 0.1 broadcast_bitcast_fusion
  1.4 0.8 or_select_fusion
  2.2 0.6 reshape.17.lse
  2.8 0.7 bitcast_subtract_fusion
  3.5 0.6 reshape.18.local
  4.1 78.1 %shard_map.94 = (bf16[1536,512]{1,0:T(8,128)(2,1)}, bf16[64,512]{1,0:T(8,128)(2,1)}, bf16[64,512]{1,0:T(8,128)(2,1)}) custom-call(bf16[1536,512]{1,0:T(8,128)(2,1)} %queries.1, bf16[1536,512]{1,0:T(8,128)(2,1)} %grads.1, bf16[512,512]{1,0:T(8,128)(2,1)} %keys.1, bf16[512,512]{1,0:T(8,128)(2,1)} %values.1, f32[12,256]{1,0:T(8,128)} %reshape.17.lse, ...), custom_call_target="tpu_custom_call" | custom-call | tf_op jit(solution)/shard_map/pallas_call | solution.py:273
  82.2 0.0 copy-start.1
  82.2 0.0 copy-start
  82.2 2.7 %copy.17 = bf16[1536,512]{1,0:T(8,128)(2,1)} copy(bf16[1536,512]{1,0:T(8,128)(2,1)} %get-tuple-element.6) | data formatting | bytes 3145728
  84.9 0.0 copy-done.1
  84.9 0.6 copy.18
  85.5 0.0 copy-done
  85.6 0.6 copy.19
  (2 shorter events, 0.0 us)
Async XLA Ops:
  82.2 2.7 %copy-start.1 = (bf16[64,512]{1,0:T(8,128)(2,1)S(1)}, bf16[64,512]{1,0:T(8,128)(2,1)}, u32[]{:S(2)}) copy-start(bf16[64,512]{1,0:T(8,128)(2,1)} %get-tuple-element.7) | copy-start | bytes 196612
  82.2 3.3 %copy-start = (bf16[64,512]{1,0:T(8,128)(2,1)S(1)}, bf16[64,512]{1,0:T(8,128)(2,1)}, u32[]{:S(2)}) copy-start(bf16[64,512]{1,0:T(8,128)(2,1)} %get-tuple-element.8) | copy-start | bytes 196612

commit v3 on v2

v3 whole, which is shorter than its diff:
```python
import jax
import jax.numpy as jnp
from jax import lax
from jax.experimental import pallas as pl
from jax.experimental.pallas import tpu as pltpu
from jax.sharding import PartitionSpec as P

ZH, Y, CORES, ZL, X = 4, 8, 2, 2, 4
UP, DOWN = 4, 3
POOL_WAIT = 4
MESH = pl.DeviceIdType.MESH
VMEM = pl.BlockSpec(memory_space=pltpu.VMEM)


def place():
    val, qry = lax.axis_index("val"), lax.axis_index("qry")
    core, y, zh = val % CORES, (val // CORES) % Y, val // (CORES * Y)
    return core, y, zh, qry // X, qry % X


def device(core, y, zh, zl, x):
    return ((zh * Y + y) * CORES + core, zl * X + x)


def neighbours():
    core, y, zh, zl, x = place()
    across = device(1 - core, y, zh, zl, x)
    along_y = [device(core, (y + d) % Y, zh, zl, x) for d in range(1, Y)]
    along_z = [device(core, y, (zh + d) % ZH, zl, x) for d in range(1, ZH)]
    along_x = [device(core, y, zh, zl, (x + d) % X) for d in range(1, X)]
    beside = device(core, y, zh, 1 - zl, x)
    return across, along_y, along_z, along_x, beside


def mult(first, size):
    return pl.ds(pl.multiple_of(first, size), size)


def dot(a, b, dims):
    return lax.dot_general(a, b, ((dims[:1], dims[1:]), ((), ())), preferred_element_type=jnp.float32)


def push(src, dst, send, recv, there):
    copy = pltpu.make_async_remote_copy(
        src_ref=src, dst_ref=dst, send_sem=send, recv_sem=recv, device_id=there, device_id_type=MESH
    )
    copy.start()
    return copy


def backward_kernel(
    queries, grads, keys, values, lse, targets, compat, query_out, key_out, value_out,
    probs, weights, delta, delta_core, delta_sum, delta_y, delta_line, delta_z, query, sums, pool,
    from_core, up_in, down_in, up_out, down_out, sum_y, from_z, mine, line, whole,
    from_x, sum_x, from_beside, send, recv,
):
    f32, low = jnp.float32, jnp.bfloat16
    core, y, zh, zl, x = place()
    across, along_y, along_z, along_x, beside = neighbours()
    upper, lower = along_y[0], along_y[-1]
    friends = [across] + along_y + along_z + along_x + [beside]
    barrier = pltpu.get_barrier_semaphore()
    for there in friends:
        pl.semaphore_signal(barrier, inc=1, device_id=there, device_id_type=MESH)

    heads, per_head, tile = delta.shape
    count, columns = queries.shape
    value_count = keys.shape[0]
    head_width = columns // heads
    scale = head_width ** (-0.5)
    half = from_core.shape[1]
    piece = half // Y
    part = piece // ZH
    share = key_out.shape[0]
    offset = lax.axis_index("val") * value_count
    done = []
    used = iter(range(send.shape[0]))

    def start(src, dst, there):
        n = next(used)
        copy = push(src, dst, send.at[n], recv.at[n], there)
        done.append(copy)
        return copy

    def head_columns(h):
        return pl.ds(h * head_width, head_width)

    def first_pass(h, low_tile, high_tile):
        cols = head_columns(h)

        def step(b, carry):
            rows = mult(b * tile, tile)
            grad_tile = grads[rows, cols]
            local = targets[pl.ds(h, 1), rows] - offset
            mark = jnp.full(local.shape, compat[h, b], jnp.int32)
            usable = (mark == 1) | ((local >= 0) & (local < value_count))
            lse_row = jnp.where(usable, lse[pl.ds(h, 1), rows], 3e38)
            scores = dot(keys[:, cols], queries[rows, cols], (1, 1)) * scale
            p = jnp.exp(scores - lse_row)
            dprobs = dot(values[:, cols], grad_tile, (1, 1))
            terms = p * dprobs
            delta[h, pl.ds(b, 1), :] = jnp.sum(terms, axis=0, keepdims=True)
            hit = lax.broadcasted_iota(jnp.int32, p.shape, 0) == local
            probs[h, :, rows] = p
            weights[h, :, rows] = terms + p - jnp.where(hit, 1.0, 0.0)
            sums[1, h] += dot(p.astype(low), grad_tile, (1, 0))
            return carry

        lax.fori_loop(low_tile, high_tile, step, 0)

    def second_pass(h, low_tile, high_tile):
        cols = head_columns(h)

        def step(b, carry):
            rows = mult(b * tile, tile)
            d = delta_core[h, pl.ds(b, 1), :]
            dscores = (weights[h, :, rows] - probs[h, :, rows] * d).astype(low)
            query[h, rows, :] = (dot(dscores, keys[:, cols], (0, 0)) * scale).astype(low)
            sums[0, h] += dot(dscores, queries[rows, cols], (1, 0))
            return carry

        lax.fori_loop(low_tile, high_tile, step, 0)

    def delta_steps(h):
        swap = start(delta.at[h], delta_core.at[h], across)
        yield
        swap.wait_recv()
        delta_sum[h] = delta[h] + delta_core[h]
        stage = [start(delta_sum.at[h], delta_y.at[h, d], there) for d, there in enumerate(along_y)]
        yield
        acc = delta_sum[h]
        for d, copy in enumerate(stage):
            copy.wait_recv()
            acc = acc + delta_y[h, d]
        delta_line[h] = acc
        stage = [start(delta_line.at[h], delta_z.at[h, d], there) for d, there in enumerate(along_z)]
        yield
        for d, copy in enumerate(stage):
            copy.wait_recv()
            acc = acc + delta_z[h, d]
        delta_core[h] = acc

    def pool_steps(n, h, out, factor, wait):
        for r in range(ZL * X):
            pool[n, h, r // X, r % X] = (sums[n, h, pl.ds(r * share, share), :] * factor).astype(low)
        x_stage = [
            start(pool.at[n, h, :, (x + d) % X], from_x.at[n, h, d - 1], there)
            for d, there in zip(range(1, X), along_x)
        ]
        for _ in range(wait):
            yield
        acc = pool[n, h, :, x].astype(f32)
        for d, copy in enumerate(x_stage):
            copy.wait_recv()
            acc = acc + from_x[n, h, d].astype(f32)
        sum_x[n, h] = acc.astype(low)
        copy = start(sum_x.at[n, h, 1 - zl], from_beside.at[n, h], beside)
        for _ in range(3):
            yield
        copy.wait_recv()
        out[:, head_columns(h)] = (sum_x[n, h, zl].astype(f32) + from_beside[n, h].astype(f32)).astype(low)

    def query_steps(h):
        cols = head_columns(h)

        def rows(c, owner):
            return mult(c * half + lax.rem(owner + Y, Y) * piece, piece)

        def own(owner):
            inside = mult(lax.rem(owner + Y, Y) * piece, piece)
            return query[h, rows(core, owner), :].astype(f32) + from_core[h, inside, :].astype(f32)

        swap = start(query.at[h, mult((1 - core) * half, half)], from_core.at[h], across)
        yield
        swap.wait_recv()
        up_out[h, 0] = own(y + UP).astype(low)
        up = start(up_out.at[h, 0], up_in.at[h, 0], upper)
        down_out[h, 0] = own(y - DOWN).astype(low)
        down = start(down_out.at[h, 0], down_in.at[h, 0], lower)
        for s in range(1, UP):
            yield
            up.wait_recv()
            up_out[h, s] = (own(y + UP - s) + up_in[h, s - 1].astype(f32)).astype(low)
            up = start(up_out.at[h, s], up_in.at[h, s], upper)
            if s < DOWN:
                down.wait_recv()
                down_out[h, s] = (own(y - DOWN + s) + down_in[h, s - 1].astype(f32)).astype(low)
                down = start(down_out.at[h, s], down_in.at[h, s], lower)
        yield
        down.wait_recv()
        up.wait_recv()
        total = own(y) + up_in[h, UP - 1].astype(f32) + down_in[h, DOWN - 1].astype(f32)
        for r in range(ZH):
            sum_y[h, r] = total[r * part : (r + 1) * part].astype(low)
        z_stage = [
            start(sum_y.at[h, (zh + d) % ZH], from_z.at[h, d - 1], there)
            for d, there in zip(range(1, ZH), along_z)
        ]
        yield
        acc = sum_y[h, zh].astype(f32)
        for d, copy in enumerate(z_stage):
            copy.wait_recv()
            acc = acc + from_z[h, d].astype(f32)
        mine[h] = acc.astype(low)
        back_z = [start(mine.at[h], line.at[h, zh], there) for there in along_z]
        line[h, zh] = mine[h]
        yield
        for copy in back_z:
            copy.wait_recv()
        whole[h] = jnp.concatenate([line[h, r].astype(f32) for r in range(ZH)], axis=0).astype(low)
        here = query_out.at[rows(core, y), cols]
        up = start(whole.at[h], here, upper)
        down = start(whole.at[h], here, lower)
        back_core = [start(whole.at[h], here, across)]
        query_out[rows(core, y), cols] = whole[h]
        for s in range(1, UP + 1):
            yield
            up.wait_recv()
            got = query_out.at[rows(core, y - s), cols]
            if s < UP:
                up = start(got, got, upper)
            forward = [got]
            if s <= DOWN:
                down.wait_recv()
                got = query_out.at[rows(core, y + s), cols]
                if s < DOWN:
                    down = start(got, got, lower)
                forward.append(got)
            back_core += [start(got, got, across) for got in forward]
        yield
        for copy in back_core:
            copy.wait_recv()

    sums[...] = jnp.zeros_like(sums)
    mid = per_head // 2
    first_pass(0, 0, per_head)
    pl.semaphore_wait(barrier, len(friends))
    delta_lane = delta_steps(0)
    next(delta_lane)
    lanes = [pool_steps(1, 0, value_out, 1.0, 2)]
    next(lanes[0])
    first_pass(1, 0, mid)
    next(delta_lane)
    first_pass(1, mid, per_head)
    later_lane = delta_steps(1)
    next(later_lane)
    next(delta_lane)
    lanes.append(pool_steps(1, 1, value_out, 1.0, 2))
    next(lanes[1])
    next(later_lane)
    next(delta_lane, None)
    second_pass(0, 0, per_head)
    ahead = query_steps(0)
    next(ahead)
    next(later_lane)
    lanes.append(pool_steps(0, 0, key_out, scale, POOL_WAIT))
    next(lanes[2])
    next(ahead)
    next(later_lane, None)
    for b in range(0, per_head, 2):
        second_pass(1, b, b + 2)
        if b + 2 < per_head:
            next(ahead)
    behind = query_steps(1)
    next(behind)
    lanes = [ahead, behind] + lanes + [pool_steps(0, 1, key_out, scale, POOL_WAIT)]
    while lanes:
        lanes = [steps for steps in lanes if next(steps, lanes) is not lanes]
    for copy in done:
        copy.wait_send()


def on_device(queries, pool_keys, pool_values, out_grad, lse, compat, targets):
    heads, _, query_blocks = compat.shape
    count, columns = queries.shape
    value_count = pool_keys.shape[0]
    low, f32 = jnp.bfloat16, jnp.float32
    share = value_count // (ZL * X)
    half = count // CORES
    piece = half // Y
    part = piece // ZH
    wide = columns // heads
    copies = heads * (1 + (Y - 1) + (ZH - 1) * 2 + (Y - 1) + Y + 2 * X + 1 + (Y - 1) + (ZH - 1))
    row = (query_blocks, count // query_blocks)
    return pl.pallas_call(
        backward_kernel,
        out_shape=(
            jax.ShapeDtypeStruct(queries.shape, low),
            jax.ShapeDtypeStruct((share, columns), low),
            jax.ShapeDtypeStruct((share, columns), low),
        ),
        in_specs=[VMEM] * 6 + [pl.BlockSpec(memory_space=pltpu.SMEM)],
        out_specs=(VMEM, VMEM, VMEM),
        scratch_shapes=[
            pltpu.VMEM((heads, value_count, count), f32),
            pltpu.VMEM((heads, value_count, count), f32),
            pltpu.VMEM((heads, *row), f32),
            pltpu.VMEM((heads, *row), f32),
            pltpu.VMEM((heads, *row), f32),
            pltpu.VMEM((heads, Y - 1, *row), f32),
            pltpu.VMEM((heads, *row), f32),
            pltpu.VMEM((heads, ZH - 1, *row), f32),
            pltpu.VMEM((heads, count, wide), low),
            pltpu.VMEM((2, heads, value_count, wide), f32),
            pltpu.VMEM((2, heads, ZL, X, share, wide), low),
            pltpu.VMEM((heads, half, wide), low),
            pltpu.VMEM((heads, UP, piece, wide), low),
            pltpu.VMEM((heads, DOWN, piece, wide), low),
            pltpu.VMEM((heads, UP, piece, wide), low),
            pltpu.VMEM((heads, DOWN, piece, wide), low),
            pltpu.VMEM((heads, ZH, part, wide), low),
            pltpu.VMEM((heads, ZH - 1, part, wide), low),
            pltpu.VMEM((heads, part, wide), low),
            pltpu.VMEM((heads, ZH, part, wide), low),
            pltpu.VMEM((heads, piece, wide), low),
            pltpu.VMEM((2, heads, X - 1, ZL, share, wide), low),
            pltpu.VMEM((2, heads, ZL, share, wide), low),
            pltpu.VMEM((2, heads, share, wide), low),
            pltpu.SemaphoreType.DMA((copies,)),
            pltpu.SemaphoreType.DMA((copies,)),
        ],
        compiler_params=pltpu.CompilerParams(
            collective_id=0, has_side_effects=True, vmem_limit_bytes=56 * 1024 * 1024
        ),
    )(queries, out_grad, pool_keys, pool_values, lse, jnp.transpose(targets), compat[:, 0, :])


def solution(mesh):
    placed = (
        P("qry", None),
        P("val", None),
        P("val", None),
        P("qry", None),
        P(None, "qry"),
        P(None, "val", "qry"),
        P("qry", None),
    )
    return jax.shard_map(
        on_device,
        mesh=mesh,
        in_specs=placed,
        out_specs=(P("qry", None), P(("val", "qry"), None), P(("val", "qry"), None)),
        check_vma=False,
    )
```

time: 86.5 us -> 90.8 us (1.050)
  Pallas kernels: 78.1 us -> 86 us
  other arithmetic: 2.17 us -> 0 us
  local copies, waits for them, and re-layouts: 5.29 us -> 3.95 us
    pallas_call x1, Pallas kernels: 78.1 us -> 86 us  [on_device(): pl.pallas_call(backward_kernel, out_shape=(jax.ShapeDtypeStruct(queries.s...]
    reshape x2 -> x0, local copies, waits for them, and re-layouts: 1.24 us -> none  [the longest x1 0.62 us: on_device(): local = (wanted - val * value_count).reshape(tiles, query_block)]
    unnamed x10 -> x7, local copies, waits for them, and re-layouts: 4.05 us -> 3.95 us
where the time goes in v3:
time: 90.8 us; the launch traced here: 90.6 us
  Pallas kernels  86 us (95%)
  local copies, waits for them, and re-layouts  3.95 us (4%)
    pallas_call x1, Pallas kernels, on_device(): pl.pallas_call(backward_kernel, out_shape=(jax.ShapeDtypeStruct(queries.s...  86 us
    unnamed x7, local copies, waits for them, and re-layouts  3.95 us

profile of v3, /device:TPU:1, one launch (start us, length us, event | category | flops | bytes accessed | tf_op | source)
XLA Modules:
  0.0 90.6 jit_solution(2336914985212978675)
XLA Ops:
  0.6 86.0 %shard_map.94 = (bf16[1536,512]{1,0:T(8,128)(2,1)}, bf16[64,512]{1,0:T(8,128)(2,1)}, bf16[64,512]{1,0:T(8,128)(2,1)}) custom-call(bf16[1536,512]{1,0:T(8,128)(2,1)} %queries.1, bf16[1536,512]{1,0:T(8,128)(2,1)} %grads.1, bf16[512,512]{1,0:T(8,128)(2,1)} %keys.1, bf16[512,512]{1,0:T(8,128)(2,1)} %values.1, f32[2,1536]{1,0:T(2,128)} %lse.1, ...), custom_call_target="tpu_custom_call" | custom-call | tf_op jit(solution)/shard_map/pallas_call | solution.py:285
  86.6 0.0 copy-start.1
  86.6 0.0 copy-start
  86.7 2.7 %copy.13 = bf16[1536,512]{1,0:T(8,128)(2,1)} copy(bf16[1536,512]{1,0:T(8,128)(2,1)} %get-tuple-element.6) | data formatting | bytes 3145728
  89.3 0.0 copy-done.1
  89.3 0.6 copy.14
  90.0 0.0 copy-done
  90.0 0.6 copy.15
Async XLA Ops:
  86.6 2.7 %copy-start.1 = (bf16[64,512]{1,0:T(8,128)(2,1)S(1)}, bf16[64,512]{1,0:T(8,128)(2,1)}, u32[]{:S(2)}) copy-start(bf16[64,512]{1,0:T(8,128)(2,1)} %get-tuple-element.7) | copy-start | bytes 196612
  86.6 3.3 %copy-start = (bf16[64,512]{1,0:T(8,128)(2,1)S(1)}, bf16[64,512]{1,0:T(8,128)(2,1)}, u32[]{:S(2)}) copy-start(bf16[64,512]{1,0:T(8,128)(2,1)} %get-tuple-element.8) | copy-start | bytes 196612

commit v4 on v2

--- a/solution.py
+++ b/solution.py
@@ -49,7 +49,7 @@
 
 
 def backward_kernel(
-    queries, grads, keys, values, lse, local, query_out, key_out, value_out,
+    queries, grads, keys, values, lse, targets, compat, query_out, key_out, value_out,
     probs, weights, delta, delta_core, delta_sum, delta_y, delta_line, delta_z, query, sums, key_sums, pool,
     from_core, up_in, down_in, up_out, down_out, sum_y, from_z, mine, line,
     from_x, sum_x, from_beside, send, recv,
@@ -64,7 +64,9 @@
         pl.semaphore_signal(barrier, inc=1, device_id=there, device_id_type=MESH)
 
     count, columns = queries.shape
-    tiles, tile = lse.shape
+    tiles, tile = delta.shape
+    value_count = keys.shape[0]
+    offset = lax.axis_index("val") * value_count
     heads = probs.shape[0]
     head_width = columns // heads
     per_head = tiles // heads
@@ -93,19 +95,23 @@
         def first_pass(b, carry):
             rows = mult(b * tile, tile)
             grad_tile = grads[rows, cols]
+            local = targets[pl.ds(h, 1), rows] - offset
+            mark = jnp.full(local.shape, compat[h, b], jnp.int32)
+            usable = (mark == 1) | ((local >= 0) & (local < value_count))
+            lse_row = jnp.where(usable, lse[pl.ds(h, 1), rows], 3e38)
             scores = dot(keys[:, cols], queries[rows, cols], (1, 1)) * scale
-            p = jnp.exp(scores - lse[pl.ds(h * per_head + b, 1), :])
+            p = jnp.exp(scores - lse_row)
             dprobs = dot(values[:, cols], grad_tile, (1, 1))
             terms = p * dprobs
             delta[pl.ds(h * per_head + b, 1), :] = jnp.sum(terms, axis=0, keepdims=True)
             slot = lax.broadcasted_iota(jnp.int32, p.shape, 0)
-            hit = slot == local[pl.ds(h * per_head + b, 1), :]
+            hit = slot == local
             probs[h, :, rows] = p
             weights[h, :, rows] = terms + p - jnp.where(hit, 1.0, 0.0)
             sums[...] += dot(p.astype(low), grad_tile, (1, 0))
             return carry
 
-        lax.fori_loop(0, per_head, first_pass, 0)
+        lax.fori_loop(0, per_head, first_pass, 0, unroll=3)
         for r in range(ZL * X):
             pool[1, r // X, r % X, :, cols] = sums[pl.ds(r * share, share), :].astype(low)
 
@@ -233,7 +239,7 @@
             return carry
 
         per_chunk = per_head // CHUNKS
-        lax.fori_loop(k * per_chunk, (k + 1) * per_chunk, step, 0)
+        lax.fori_loop(k * per_chunk, (k + 1) * per_chunk, step, 0, unroll=3)
 
     key_sums[...] = jnp.zeros_like(key_sums)
     lanes = [value_lane]
@@ -252,18 +258,12 @@
 
 
 def on_device(queries, pool_keys, pool_values, out_grad, lse, compat, targets):
-    heads, value_blocks, query_blocks = compat.shape
+    heads, _, query_blocks = compat.shape
     count, columns = queries.shape
     value_count = pool_keys.shape[0]
-    val = lax.axis_index("val")
     query_block = count // query_blocks
     tiles = heads * query_blocks
     low, f32 = jnp.bfloat16, jnp.float32
-    wanted = jnp.transpose(targets)
-    marks = jnp.repeat(compat[:, 0, :], query_block, axis=1)
-    usable = (marks == 1) | (wanted // value_count == val)
-    lse_rows = jnp.where(usable, lse, 3e38).reshape(tiles, query_block)
-    local = (wanted - val * value_count).reshape(tiles, query_block)
     share = value_count // (ZL * X)
     half = count // (CORES * CHUNKS)
     piece = half // Y
@@ -277,7 +277,7 @@
             jax.ShapeDtypeStruct((share, columns), low),
             jax.ShapeDtypeStruct((share, columns), low),
         ),
-        in_specs=[VMEM] * 6,
+        in_specs=[VMEM] * 6 + [pl.BlockSpec(memory_space=pltpu.SMEM)],
         out_specs=(VMEM, VMEM, VMEM),
         scratch_shapes=[
             pltpu.VMEM((heads, value_count, count), f32),
@@ -310,7 +310,7 @@
         compiler_params=pltpu.CompilerParams(
             collective_id=0, has_side_effects=True, vmem_limit_bytes=56 * 1024 * 1024
         ),
-    )(queries, out_grad, pool_keys, pool_values, lse_rows, local)
+    )(queries, out_grad, pool_keys, pool_values, lse, jnp.transpose(targets), compat[:, 0, :])
 
 
 def solution(mesh):

time: 86.5 us -> 79.1 us (0.914)
  Pallas kernels: 78.1 us -> 74.3 us
  other arithmetic: 2.17 us -> 0 us
  local copies, waits for them, and re-layouts: 5.29 us -> 3.95 us
    pallas_call x1, Pallas kernels: 78.1 us -> 74.3 us  [on_device(): pl.pallas_call(backward_kernel, out_shape=(jax.ShapeDtypeStruct(queries.s...]
    reshape x2 -> x0, local copies, waits for them, and re-layouts: 1.24 us -> none  [the longest x1 0.62 us: on_device(): local = (wanted - val * value_count).reshape(tiles, query_block)]
    unnamed x10 -> x7, local copies, waits for them, and re-layouts: 4.05 us -> 3.95 us
where the time goes in v4:
time: 79.1 us; the launch traced here: 78.9 us
  Pallas kernels  74.3 us (94%)
  local copies, waits for them, and re-layouts  3.95 us (5%)
    pallas_call x1, Pallas kernels, on_device(): pl.pallas_call(backward_kernel, out_shape=(jax.ShapeDtypeStruct(queries.s...  74.3 us
    unnamed x7, local copies, waits for them, and re-layouts  3.95 us

profile of v4, /device:TPU:1, one launch (start us, length us, event | category | flops | bytes accessed | tf_op | source)
XLA Modules:
  0.0 78.9 jit_solution(13364645521783932269)
XLA Ops:
  0.6 74.3 %shard_map.94 = (bf16[1536,512]{1,0:T(8,128)(2,1)}, bf16[64,512]{1,0:T(8,128)(2,1)}, bf16[64,512]{1,0:T(8,128)(2,1)}) custom-call(bf16[1536,512]{1,0:T(8,128)(2,1)} %queries.1, bf16[1536,512]{1,0:T(8,128)(2,1)} %grads.1, bf16[512,512]{1,0:T(8,128)(2,1)} %keys.1, bf16[512,512]{1,0:T(8,128)(2,1)} %values.1, f32[2,1536]{1,0:T(2,128)} %lse.1, ...), custom_call_target="tpu_custom_call" | custom-call | tf_op jit(solution)/shard_map/pallas_call | solution.py:273
  75.0 0.0 copy-start.1
  75.0 0.0 copy-start
  75.0 2.7 %copy.13 = bf16[1536,512]{1,0:T(8,128)(2,1)} copy(bf16[1536,512]{1,0:T(8,128)(2,1)} %get-tuple-element.6) | data formatting | bytes 3145728
  77.7 0.0 copy-done.1
  77.7 0.6 copy.14
  78.3 0.0 copy-done
  78.3 0.6 copy.15
Async XLA Ops:
  75.0 2.7 %copy-start.1 = (bf16[64,512]{1,0:T(8,128)(2,1)S(1)}, bf16[64,512]{1,0:T(8,128)(2,1)}, u32[]{:S(2)}) copy-start(bf16[64,512]{1,0:T(8,128)(2,1)} %get-tuple-element.7) | copy-start | bytes 196612
  75.0 3.3 %copy-start = (bf16[64,512]{1,0:T(8,128)(2,1)S(1)}, bf16[64,512]{1,0:T(8,128)(2,1)}, u32[]{:S(2)}) copy-start(bf16[64,512]{1,0:T(8,128)(2,1)} %get-tuple-element.8) | copy-start | bytes 196612

commit v5 on v4

--- a/solution.py
+++ b/solution.py
@@ -111,7 +111,7 @@
             sums[...] += dot(p.astype(low), grad_tile, (1, 0))
             return carry
 
-        lax.fori_loop(0, per_head, first_pass, 0, unroll=3)
+        lax.fori_loop(0, per_head, first_pass, 0, unroll=True)
         for r in range(ZL * X):
             pool[1, r // X, r % X, :, cols] = sums[pl.ds(r * share, share), :].astype(low)
 
@@ -246,6 +246,8 @@
     for k in range(CHUNKS):
         for h in range(heads):
             second_pass(k, h)
+            if k > 0 and h == 0:
+                next(lanes[k])
         lanes.append(query_steps(k))
         next(lanes[-1])
     for r in range(ZL * X):

time: 79.1 us -> 81.9 us (1.035)
  Pallas kernels: 74.3 us -> 77.1 us
    pallas_call x1, Pallas kernels: 74.3 us -> 77.1 us  [on_device(): pl.pallas_call(backward_kernel, out_shape=(jax.ShapeDtypeStruct(queries.s...]
where the time goes in v5:
time: 81.9 us; the launch traced here: 81.7 us
  Pallas kernels  77.1 us (94%)
  local copies, waits for them, and re-layouts  3.95 us (5%)
    pallas_call x1, Pallas kernels, on_device(): pl.pallas_call(backward_kernel, out_shape=(jax.ShapeDtypeStruct(queries.s...  77.1 us
    unnamed x7, local copies, waits for them, and re-layouts  3.95 us

profile of v5, /device:TPU:1, one launch (start us, length us, event | category | flops | bytes accessed | tf_op | source)
XLA Modules:
  0.0 81.7 jit_solution(9194594047851370941)
XLA Ops:
  0.6 77.1 %shard_map.94 = (bf16[1536,512]{1,0:T(8,128)(2,1)}, bf16[64,512]{1,0:T(8,128)(2,1)}, bf16[64,512]{1,0:T(8,128)(2,1)}) custom-call(bf16[1536,512]{1,0:T(8,128)(2,1)} %queries.1, bf16[1536,512]{1,0:T(8,128)(2,1)} %grads.1, bf16[512,512]{1,0:T(8,128)(2,1)} %keys.1, bf16[512,512]{1,0:T(8,128)(2,1)} %values.1, f32[2,1536]{1,0:T(2,128)} %lse.1, ...), custom_call_target="tpu_custom_call" | custom-call | tf_op jit(solution)/shard_map/pallas_call | solution.py:275
  77.7 0.0 copy-start.1
  77.7 0.0 copy-start
  77.7 2.7 %copy.13 = bf16[1536,512]{1,0:T(8,128)(2,1)} copy(bf16[1536,512]{1,0:T(8,128)(2,1)} %get-tuple-element.6) | data formatting | bytes 3145728
  80.4 0.0 copy-done.1
  80.4 0.6 copy.14
  81.1 0.0 copy-done
  81.1 0.6 copy.15
Async XLA Ops:
  77.7 2.7 %copy-start.1 = (bf16[64,512]{1,0:T(8,128)(2,1)S(1)}, bf16[64,512]{1,0:T(8,128)(2,1)}, u32[]{:S(2)}) copy-start(bf16[64,512]{1,0:T(8,128)(2,1)} %get-tuple-element.7) | copy-start | bytes 196612
  77.7 3.3 %copy-start = (bf16[64,512]{1,0:T(8,128)(2,1)S(1)}, bf16[64,512]{1,0:T(8,128)(2,1)}, u32[]{:S(2)}) copy-start(bf16[64,512]{1,0:T(8,128)(2,1)} %get-tuple-element.8) | copy-start | bytes 196612
